TPU v7x, 32 devices: a whole 2x2x4 slice. The times are simulated.
32 devices in a mesh: bra: 8 (over z, y), ket: 4 (over x, core).
Axes of the slice: x: 2, y: 2, z: 4, core: 2. Of those that a mesh axis runs over, the one named last changes fastest.
Arguments:
- integrals: bfloat16 [256, 1024, 1024], P(('bra', 'ket')), may hold values from -0.1875 to 0.1875
- quartets: int32 [256, 4], P(('bra', 'ket')), may hold values from 0 to 127, as said below
- density: bfloat16 [128, 128, 12, 1024], P(('bra', 'ket')), may hold values from -6 to 6
- owner_map: int32 [128], replicated, may hold values from 0 to 127, each once
Outputs:
- fock_rows: bfloat16 [128, 128, 12, 1024], P(('bra', 'ket'))
Inputs may be any that keep to these rules, and one draw needn't show every extreme that they name: `quartets`: the 32 block indices in the 8 rows of one device are distinct, and one block index is the first entry of some row on every device. Block row X of density and of fock_rows is stored at row owner_map[X]; each device holds 4 consecutive storage rows, in device order.
All inputs are finite; a program needn't handle non-finite values.
Results may differ from a plain program's by a relative error of at most 0.001.
Values may be sent and summed in bfloat16 or wider, within the bound.
No kernel may reach another device: no remote copies, remote signals or barrier semaphores. Data moves between devices by JAX's collectives and lax.ppermute only.
A program may use at most 384 MiB of HBM per device.

v0:
```python
import functools
import math

import jax
import jax.numpy as jnp
from jax import lax
from jax.experimental import pallas as pl
from jax.experimental.pallas import tpu as pltpu
from jax.sharding import PartitionSpec as P

ORDER = (0, 1, 4, 2, 3, 5)
ROLE_ROW = tuple((0, 0, 1, 1, 2, 3)[role] for role in ORDER)
ROLE_COL = tuple((1, 2, 2, 3, 3, 0)[role] for role in ORDER)
ROLES = 6
PAD_N = 16
ROWS = 16
AXES = ("bra", "ket")
BF16 = jnp.bfloat16
F32 = jnp.float32
VMEM_BYTES = 60 * 1024 * 1024
READ_SLOTS = 2
FIRST_SLOTS = 4
RELAY_ROWS = 4
READ_SPARE = 8
TERM_SPARE = 16


def params(axes=1):
    return pltpu.CompilerParams(
        dimension_semantics=("arbitrary",) * axes, vmem_limit_bytes=VMEM_BYTES
    )


def cost(flops, moved):
    return pl.CostEstimate(flops=int(flops), bytes_accessed=int(moved), transcendentals=0)


def hot_rows(target, width, base=0):
    columns = lax.broadcasted_iota(jnp.int32, (target.shape[0], width), 1) + base
    return jnp.where(columns == target, 1.0, 0.0).astype(BF16)


def hot_columns(target, height, base=0):
    rows = lax.broadcasted_iota(jnp.int32, (height, target.shape[1]), 0) + base
    return jnp.where(rows == target, 1.0, 0.0).astype(BF16)


def dot_nn(left, right):
    return jnp.dot(left, right, preferred_element_type=F32)


def dot_nt(left, right):
    return lax.dot_general(left, right, (((1,), (1,)), ((), ())), preferred_element_type=F32)


def rows_per_group(slots):
    return min(4, ROWS // slots)


def tile_rows(tiles, per, blocks):
    inner = jnp.arange(per, dtype=jnp.int32)[None, :, None]
    rows = (tiles // blocks * (per * blocks) + tiles % blocks)[:, None, :] + inner * blocks
    return jnp.where(tiles[:, None, :] >= 0, rows, -1)


def slot_rows(slot, slots, dens):
    ids = jnp.arange(dens, dtype=jnp.int32)
    per = rows_per_group(slots)
    rows = (slot // slots * (dens * slots) + slot % slots)[..., None]
    rows = rows + ids // per * (per * slots) + ids % per * slots
    return jnp.where(slot[..., None] >= 0, rows, -1)


def pad_rows(rows):
    pad = [(0, 0)] * (rows.ndim - 1) + [(0, PAD_N - rows.shape[-1])]
    return jnp.pad(rows, pad, constant_values=-1).reshape(-1)


def gather_body(target_ref, density_ref, *refs):
    *out_refs, hot_ref = refs
    peers, _, rows, lanes = out_refs[0].shape
    depth = hot_ref.shape[1]

    @pl.when(pl.program_id(0) == 0)
    def _():
        hot_ref[...] = hot_rows(target_ref[...], depth)

    source = density_ref[...].reshape(depth, lanes)
    half = lanes // 2
    for part in range(2):
        span = slice(part * half, (part + 1) * half)
        picked = dot_nn(hot_ref[...], source[:, span]).reshape(-1, rows, half)
        for which, out_ref in enumerate(out_refs):
            mine = picked[which * peers : (which + 1) * peers]
            out_ref[:, 0, :, span] = mine.astype(BF16)


def gather_tiles(wanted, density_rows):
    peers, slots = wanted[0].shape
    rows_dev, dens, blocks, lanes = density_rows.shape
    per = rows_per_group(slots)
    groups, rows = dens // per, per * slots
    depth = rows_dev * per * blocks
    target = jnp.concatenate([tile_rows(each, per, blocks).reshape(-1, 1) for each in wanted])
    out = jax.ShapeDtypeStruct((peers, groups, rows, lanes), BF16)
    return pl.pallas_call(
        gather_body,
        grid=(groups,),
        in_specs=[
            pl.BlockSpec(target.shape, lambda g: (0, 0)),
            pl.BlockSpec((rows_dev, per, blocks, lanes), lambda g: (0, g, 0, 0)),
        ],
        out_specs=[pl.BlockSpec((peers, 1, rows, lanes), lambda g: (0, g, 0, 0))] * len(wanted),
        out_shape=[out] * len(wanted),
        scratch_shapes=[pltpu.VMEM((target.shape[0], depth), BF16)],
        compiler_params=params(),
        name="gather_tiles",
    )(target, density_rows)


def pick_body(*refs, relay, swapped, based):
    if relay:
        relay_target_ref, relayed_ref, *refs = refs
    if based:
        base_ref, *refs = refs
    if swapped:
        swap_ref, *refs = refs
    target_ref, slots_ref, out_ref, total_ref = refs
    step = pl.program_id(0)
    depth = slots_ref.shape[0]

    def fresh():
        total = dot_nn(hot_rows(target_ref[...], depth, step * depth), slots_ref[...])
        if relay:
            hot = hot_rows(relay_target_ref[...], relayed_ref.shape[0])
            total += dot_nn(hot, relayed_ref[...])
        elif based:
            total += base_ref[...].astype(F32)
        return total

    def finish(total):
        if not swapped:
            total = total.reshape(out_ref.shape)
            out_ref[...] = total.astype(BF16)
            return
        half = out_ref.shape[0] // 2
        out_ref[:half, :] = total[:half, :].astype(BF16)
        out_ref[half:, :] = dot_nn(total[half:, :].astype(BF16), swap_ref[...]).astype(BF16)

    if total_ref.shape[0] == 8:
        finish(fresh())
        return

    @pl.when(step == 0)
    def _():
        total_ref[...] = fresh()

    @pl.when(step > 0)
    def _():
        hot = hot_rows(target_ref[...], depth, step * depth)
        total_ref[...] += dot_nn(hot, slots_ref[...])

    @pl.when(step == pl.num_programs(0) - 1)
    def _():
        finish(total_ref[...])


def pick_rows(row_of, received, swap=None, relay_row_of=None, relayed=None, base=None, shape=None):
    depth, lanes = received.shape
    chunk = depth
    if depth > 1536:
        chunk = math.gcd(depth, 128)
    wanted = row_of.shape[0]
    column = pl.BlockSpec((wanted, 1), lambda k: (0, 0))
    specs, operands = [], []
    if relayed is not None:
        specs += [column, pl.BlockSpec(relayed.shape, lambda k: (0, 0))]
        operands += [relay_row_of.reshape(wanted, 1), relayed]
    if base is not None:
        specs += [pl.BlockSpec(base.shape, lambda k: (0, 0))]
        operands += [base]
    if swap is not None:
        specs += [pl.BlockSpec(swap.shape, lambda k: (0, 0))]
        operands += [swap]
    return pl.pallas_call(
        functools.partial(
            pick_body,
            relay=relayed is not None,
            swapped=swap is not None,
            based=base is not None,
        ),
        grid=(depth // chunk,),
        in_specs=[*specs, column, pl.BlockSpec((chunk, lanes), lambda k: (k, 0))],
        out_specs=pl.BlockSpec(shape or (wanted, lanes), lambda k: (0,) * len(shape or (0, 0))),
        out_shape=jax.ShapeDtypeStruct(shape or (wanted, lanes), BF16),
        scratch_shapes=[pltpu.VMEM((8 if chunk == depth else wanted, lanes), F32)],
        compiler_params=params(),
        name="pick_rows",
    )(*operands, row_of.reshape(wanted, 1), received)


def exchange(read_lanes, trade, write, width):
    lanes = width * width
    blocks = lanes // 128
    low = 128 // width
    high = width // low
    for block in range(blocks):
        piece = read_lanes(block).reshape(high, low, width, 128)
        wide = jnp.concatenate(
            [piece[:, part].reshape(high * width, 128) for part in range(low)], axis=1
        )
        traded = dot_nn(wide, trade).astype(BF16)
        for part in range(low):
            group = traded[:, part * 128 : (part + 1) * 128].reshape(high, width, 128)
            for lead in range(high):
                write(block * low + part, lead, group[lead])


def regroup_body(swap_ref, trade_ref, block_ref, *refs, width):
    first_ref, second_ref, swapped_ref = refs[-3:]
    lanes = width * width
    half = lanes // 2
    for part in range(2):
        span = slice(part * half, (part + 1) * half)
        swapped_ref[:, span] = dot_nn(block_ref[0], swap_ref[:, span]).astype(BF16)

    def writer(out_ref):
        def write(row_block, lane_block, value):
            out_ref[
                0,
                row_block * width : (row_block + 1) * width,
                lane_block * 128 : (lane_block + 1) * 128,
            ] = value

        return write

    exchange(
        lambda b: swapped_ref[:, b * 128 : (b + 1) * 128],
        trade_ref[...],
        writer(first_ref),
        width,
    )
    exchange(
        lambda b: block_ref[0, :, b * 128 : (b + 1) * 128],
        trade_ref[...],
        writer(second_ref),
        width,
    )


def regroup(integrals, swap, trade, begin, end, into=(), work=1):
    count, lanes, _ = integrals.shape
    width = math.isqrt(lanes)
    whole = pl.BlockSpec((1, lanes, lanes), lambda i: (i + begin, 0, 0))
    out = jax.ShapeDtypeStruct(integrals.shape, BF16)
    return pl.pallas_call(
        functools.partial(regroup_body, width=width),
        grid=(end - begin,),
        in_specs=[
            pl.BlockSpec(swap.shape, lambda i: (0, 0)),
            pl.BlockSpec(trade.shape, lambda i: (0, 0)),
            whole,
            *[pl.BlockSpec(memory_space=pl.ANY)] * len(into),
        ],
        out_specs=[whole, whole],
        out_shape=[out, out],
        scratch_shapes=[pltpu.VMEM((lanes, lanes), BF16)],
        input_output_aliases={3 + which: which for which in range(len(into))},
        compiler_params=params(),
        cost_estimate=cost(work, work),
        name="regroup",
    )(swap, trade, integrals, *into)


def contract_body(tiles_ref, block_ref, first_ref, second_ref, high_ref, low_ref):
    block, first, second = block_ref[0], first_ref[0], second_ref[0]

    def tile(role):
        return tiles_ref[ORDER.index(role), 0]

    def put(role, term):
        top = term.astype(BF16)
        role = ORDER.index(role)
        high_ref[role, 0] = top
        low_ref[role, 0] = (term - top.astype(F32)).astype(BF16)

    put(0, 2.0 * dot_nt(tile(4), block))
    put(4, 2.0 * dot_nn(tile(0), block))
    put(1, -dot_nn(tile(3), first))
    put(3, -dot_nt(tile(1), first))
    put(2, -dot_nt(tile(5), second))
    put(5, -dot_nn(tile(2), second))


def contract(tiles, integrals, first, second):
    count, lanes, _ = integrals.shape
    whole = pl.BlockSpec((1, lanes, lanes), lambda i: (i, 0, 0))
    part = pl.BlockSpec((ROLES, 1, PAD_N, lanes), lambda i: (0, i, 0, 0))
    out = jax.ShapeDtypeStruct((ROLES, count, PAD_N, lanes), BF16)
    return pl.pallas_call(
        contract_body,
        grid=(count,),
        in_specs=[part, whole, whole, whole],
        out_specs=[part, part],
        out_shape=[out, out],
        compiler_params=params(),
        name="contract",
    )(tiles, integrals, first, second)


def pack_body(target_ref, swap_ref, high_ref, low_ref, out_ref, terms_ref):
    half = high_ref.shape[0]

    @pl.when(pl.program_id(0) == 0)
    def _():
        mid = half // 2
        for which, source in enumerate((high_ref, low_ref)):
            start = which * half
            terms_ref[start : start + mid, :] = source[:mid, :]
            swapped = dot_nn(source[mid:, :], swap_ref[...]).astype(BF16)
            terms_ref[start + mid : start + half, :] = swapped

    out_ref[...] = dot_nn(hot_rows(target_ref[...], 2 * half), terms_ref[...]).astype(BF16)


def pack_terms(row_of, swap, high, low):
    count = row_of.shape[0]
    half, lanes = high.shape
    chunk = math.gcd(count, 256 if count <= 2048 else 64)
    return pl.pallas_call(
        pack_body,
        grid=(count // chunk,),
        in_specs=[
            pl.BlockSpec((chunk, 1), lambda k: (k, 0)),
            pl.BlockSpec((lanes, lanes), lambda k: (0, 0)),
            pl.BlockSpec((half, lanes), lambda k: (0, 0)),
            pl.BlockSpec((half, lanes), lambda k: (0, 0)),
        ],
        out_specs=pl.BlockSpec((chunk, lanes), lambda k: (k, 0)),
        out_shape=jax.ShapeDtypeStruct((count, lanes), BF16),
        scratch_shapes=[pltpu.VMEM((2 * half, lanes), BF16)],
        compiler_params=params(),
        name="pack_terms",
    )(row_of.reshape(count, 1), swap, high, low)


def scatter_body(*refs, relay):
    if relay:
        relay_target_ref, relayed_ref, *refs, relay_hot_ref = refs
    target_ref, slots_ref, out_ref, hot_ref = refs
    rows_dev, per, blocks, lanes = out_ref.shape
    height = per * blocks
    depth = hot_ref.shape[1]

    @pl.when(pl.program_id(0) == 0)
    def _():
        hot_ref[...] = hot_columns(target_ref[...], rows_dev * height)
        if relay:
            for part in range(relay_hot_ref.shape[0]):
                target = relay_target_ref[part : part + 1, :]
                relay_hot_ref[part] = hot_columns(target, rows_dev * height)

    slots = slots_ref[...].reshape(depth, lanes)
    for row in range(rows_dev):
        span = slice(row * height, (row + 1) * height)
        total = dot_nn(hot_ref[span, :], slots)
        if relay:
            part = pl.program_id(0) % relay_hot_ref.shape[0]
            relayed = relayed_ref[...].astype(F32).reshape(-1, lanes).astype(BF16)
            total += dot_nn(relay_hot_ref[part, span, :], relayed)
        out_ref[row] = total.astype(BF16).reshape(per, blocks, lanes)


def scatter_split(slots):
    return max(slots, 8)


def landing_rows(landing, blocks):
    slots = landing.shape[1]
    return tile_rows(landing, scatter_split(slots) // slots, blocks).reshape(1, -1)


def relay_landing_rows(landing, slots, blocks):
    per = scatter_split(slots) // slots
    inner = jnp.arange(RELAY_ROWS, dtype=jnp.int32)
    rows = (landing // blocks * (per * blocks) + landing % blocks)[:, None] + inner % per * blocks
    kind = jnp.arange(RELAY_ROWS // per, dtype=jnp.int32)[:, None, None]
    rows = jnp.where((landing[:, None] >= 0) & (inner // per == kind), rows, -1)
    return rows.reshape(kind.shape[0], -1)


def scatter_terms(target, arrived, slots, rows_dev, blocks, relay_target=None, relayed=None):
    peers, groups, rows, lanes = arrived.shape
    split = scatter_split(slots)
    steps, per = groups * rows // split, split // slots
    high = rows_dev * per * blocks
    specs, operands = [], []
    scratch = [pltpu.VMEM((high, peers * split), BF16)]
    if relayed is not None:
        depth = peers * RELAY_ROWS
        kinds = relay_target.shape[0]
        specs = [
            pl.BlockSpec((kinds, depth), lambda g: (0, 0)),
            pl.BlockSpec((peers, 1, RELAY_ROWS, lanes), lambda g: (0, g // kinds, 0, 0)),
        ]
        operands = [relay_target, relayed]
        scratch += [pltpu.VMEM((kinds, high, depth), BF16)]
    return pl.pallas_call(
        functools.partial(scatter_body, relay=relayed is not None),
        grid=(steps,),
        in_specs=[
            *specs,
            pl.BlockSpec((1, peers * split), lambda g: (0, 0)),
            pl.BlockSpec((peers, 1, split, lanes), lambda g: (0, g, 0, 0)),
        ],
        out_specs=pl.BlockSpec((rows_dev, per, blocks, lanes), lambda g: (0, g, 0, 0)),
        out_shape=jax.ShapeDtypeStruct((rows_dev, steps * per, blocks, lanes), BF16),
        scratch_shapes=scratch,
        compiler_params=params(),
        name="scatter_terms",
    )(*operands, target, arrived.reshape(peers, steps, split, lanes))


def route_body(
    me_ref, list_ref, state_hbm, out_ref, sent_ref, passed_ref, landed_ref, state_ref, sem,
    *, spare, begin, tag, span, caps, outward
):
    peers = list_ref.shape[0]
    second = peers * peers
    copy = pltpu.make_async_copy(state_hbm, state_ref, sem)
    copy.start()
    me = me_ref[0]

    for ref in (sent_ref, passed_ref, landed_ref):

        def clear(index, carry, ref=ref):
            ref[index] = -1
            return carry

        lax.fori_loop(0, ref.shape[0], clear, 0, unroll=8)
    copy.wait()

    def first_at(source, middle):
        return source * peers + middle if outward else middle * peers + source

    def one(row, place, failed):
        value = list_ref[row, begin + place]
        other = value // (span * tag)
        source, last = (row, other) if outward else (other, row)

        def search(carry):
            tries, middle, found = carry
            full = state_ref[first_at(source, middle)] >= caps[0]
            taken = state_ref[second + last * peers + middle] >= caps[1]
            found = jnp.where(full | taken, found, middle)
            following = jnp.where(middle + 1 == peers, 0, middle + 1)
            return tries + 1, following, found

        start = source + last
        start = jnp.where(start >= peers, start - peers, start)
        _, _, found = lax.while_loop(
            lambda carry: (carry[0] < peers) & (carry[2] < 0),
            search,
            (jnp.int32(0), start, jnp.int32(-1)),
        )
        index = row * spare + place
        out_ref[index] = -1

        @pl.when(found >= 0)
        def _():
            first_state, then_state = first_at(source, found), second + last * peers + found
            first, then = state_ref[first_state], state_ref[then_state]
            out_ref[index] = found * caps[1] + then
            state_ref[first_state] = first + 1
            state_ref[then_state] = then + 1
            tile = value // tag - me * span

            @pl.when(source == me)
            def _():
                sent_ref[found * caps[0] + first] = value % tag if outward else tile

            @pl.when(found == me)
            def _():
                passed_ref[last * caps[1] + then] = source * caps[0] + first

            @pl.when(last == me)
            def _():
                landed_ref[found * caps[1] + then] = tile if outward else value % tag

        return failed + jnp.where(found < 0, 1, 0)

    def each(row, failed):
        count = jnp.minimum(list_ref[row, begin + spare], spare)
        return lax.fori_loop(0, count, functools.partial(lambda p, f, r: one(r, p, f), r=row), failed)

    out_ref[peers * spare] = lax.fori_loop(0, peers, each, jnp.int32(0))


def route(me, table, begin, spare, first, second, caps, tag, span, outward):
    peers = table.shape[0]
    state = jnp.concatenate([first, second]).reshape(-1)
    smem = pl.BlockSpec(memory_space=pltpu.SMEM)
    counts = (peers * spare + 1, peers * caps[0], peers * caps[1], peers * caps[1])
    out, sent, passed, landed = pl.pallas_call(
        functools.partial(
            route_body, spare=spare, begin=begin, tag=tag, span=span, caps=caps, outward=outward
        ),
        in_specs=[smem, smem, pl.BlockSpec(memory_space=pl.ANY)],
        out_specs=[smem] * 4,
        out_shape=[jax.ShapeDtypeStruct((count,), jnp.int32) for count in counts],
        scratch_shapes=[pltpu.SMEM((2 * peers * peers,), jnp.int32), pltpu.SemaphoreType.DMA],
        name="route",
    )(me[None], table, state)
    return sent.reshape(peers, caps[0]), passed, landed, out[-1]


def tile_keys(quartets, owner_map):
    blocks = owner_map.shape[0]
    row_blocks = jnp.stack([quartets[:, pick] for pick in ROLE_ROW]).reshape(-1)
    col_blocks = jnp.stack([quartets[:, pick] for pick in ROLE_COL]).reshape(-1)
    ids = jnp.arange(blocks, dtype=jnp.int32)
    storage = jnp.sum(jnp.where(row_blocks[:, None] == ids, owner_map, 0), axis=-1)
    return storage * blocks + col_blocks


def earlier(flags):
    ids = jnp.arange(flags.shape[-1])
    ahead = ids[:, None] < ids[None, :]
    return jnp.sum((flags[..., :, None] & ahead).astype(jnp.int32), axis=-2)


def choose(hit, values, axis):
    return jnp.sum(jnp.where(hit, values + 1, 0), axis=axis) - 1


def spilled(flags, values, spare):
    place = earlier(flags)
    hit = flags[..., None] & (place[..., None] == jnp.arange(spare))
    return choose(hit, values[..., None], -2), jnp.sum(flags.astype(jnp.int32), axis=-1)


def permutation_tables(width):
    lanes = width * width
    low = 128 // width
    index = jnp.arange(lanes, dtype=jnp.int32)
    partner = index % width * width + index // width
    swap = (index[:, None] == partner[None, :]).astype(BF16)
    span = jnp.arange(low * 128, dtype=jnp.int32)
    lead, group, inner = span // 128, span % 128 // width, span % width
    partner = group * 128 + lead * width + inner
    trade = (span[None, :] == partner[:, None]).astype(BF16)
    return swap, trade


def slot_count(most):
    for slots in (4, 8, 16):
        if most <= slots:
            return slots
    raise ValueError(most)


def exchange_slots(array):
    return lax.all_to_all(array, AXES, split_axis=0, concat_axis=0, tiled=True)


def slot_count(most):
    for slots in (4, 8, 16):
        if most <= slots:
            return slots
    raise ValueError(most)


def exchange_slots(array, axis=0):
    return lax.all_to_all(array, AXES, split_axis=axis, concat_axis=axis, tiled=True)


def hand_on(slot_of, received, dens):
    peers = slot_of.shape[0]
    lanes = received.shape[-1]
    shape = (peers, dens // RELAY_ROWS, RELAY_ROWS, lanes)
    rows = slot_rows(slot_of, FIRST_SLOTS, dens).reshape(-1)
    return exchange_slots(pick_rows(rows, received.reshape(-1, lanes), shape=shape))


def local(integrals, quartets, density, owner_map):
    rows_dev, blocks, dens, lanes = density.shape
    devices = lax.axis_size(AXES)
    me = lax.axis_index(AXES)
    quartet_count = quartets.shape[0]
    tile_count = ROLES * quartet_count
    span = rows_dev * blocks
    most = 2 * rows_dev
    tag = 1 << (2 * tile_count - 1).bit_length()
    device_ids = jnp.arange(devices, dtype=jnp.int32)
    tile_ids = jnp.arange(tile_count, dtype=jnp.int32)
    density_rows = jnp.transpose(density, (0, 2, 1, 3))
    swap, trade = permutation_tables(math.isqrt(lanes))

    key = tile_keys(quartets, owner_map)
    holder = key // span
    rank = jnp.sum(
        ((holder[:, None] == holder) & (tile_ids[:, None] < tile_ids)).astype(jnp.int32), axis=0
    )
    asked = jnp.sum((holder[:, None] == device_ids).astype(jnp.int32), axis=0)
    spare, spare_count = spilled(rank >= 2 * READ_SLOTS, key * tag + tile_ids, READ_SPARE)
    message = jnp.concatenate([key * 16 + rank, spare, spare_count[None], asked])
    message = jnp.pad(message, (0, -message.shape[0] % 128))
    told = exchange_slots(jnp.broadcast_to(message, (devices,) + message.shape))
    keys, ranks = told[:, :tile_count] // 16, told[:, :tile_count] % 16
    counts = told[:, tile_count + READ_SPARE + 1 :][:, :devices]
    in_second = jnp.minimum(counts, READ_SLOTS)
    in_first = jnp.minimum(counts - in_second, READ_SLOTS)
    caps = (READ_SLOTS, READ_SLOTS)
    extra, passed, landed, read_misses = route(
        me, told, tile_count, READ_SPARE, in_first, in_second, caps, tag, span, False
    )
    most_spare = jnp.max(told[:, tile_count + READ_SPARE])
    read_fits = (read_misses == 0) & (most_spare <= READ_SPARE)

    mine = keys // span == me
    local_tile = keys - me * span

    def requests(begin, slots):
        hit = mine[:, :, None] & (ranks[:, :, None] == jnp.arange(slots) + begin)
        return choose(hit, local_tile[:, :, None], 1)

    wanted = jnp.maximum(requests(READ_SLOTS, READ_SLOTS), extra)
    sent, sent_then = gather_tiles([wanted, requests(0, READ_SLOTS)], density_rows)
    received = exchange_slots(sent)
    early = quartet_count * 5 // 8
    work = 2 * lanes**3 * early
    first, second = regroup(integrals, swap, trade, 0, early, work=work)
    received, first, second = lax.optimization_barrier((received, first, second))
    passed_rows = slot_rows(passed, READ_SLOTS, dens).reshape(devices, READ_SLOTS, -1, 4)
    passed_rows = jnp.transpose(passed_rows, (0, 2, 3, 1)).reshape(-1)
    passed_on = pick_rows(
        passed_rows, received.reshape(-1, lanes), base=sent_then.reshape(-1, lanes)
    )
    received_then = exchange_slots(passed_on.reshape(sent_then.shape))
    keys, ranks, first, second, _ = lax.optimization_barrier((keys, ranks, first, second, passed_on))
    first, second = regroup(integrals, swap, trade, early, quartet_count, (first, second))

    homes = keys // span
    flat = keys.reshape(-1)
    shared = jnp.sum((flat[:, None] == flat).astype(jnp.int32), axis=0) > 1
    shared = shared.reshape(keys.shape)
    together = homes[:, :, None] == homes[:, None, :]
    before = 1 + (shared[:, :, None] & (tile_ids[:, None] < tile_ids)).astype(jnp.int32)
    low_ranks = jnp.where(shared, jnp.sum(jnp.where(together, before, 0), axis=1), -1)
    at_home = homes[:, :, None] == device_ids
    low_counts = jnp.sum((at_home & shared[:, :, None]).astype(jnp.int32), axis=1)
    both_ranks = jnp.concatenate([ranks, low_ranks], axis=1)
    values = keys * tag + tile_ids
    values = jnp.concatenate([values, values + tile_count], axis=1)
    term_list, term_counts = spilled(both_ranks >= FIRST_SLOTS, values, TERM_SPARE)
    term_table = jnp.concatenate([term_list, term_counts[:, None]], axis=1)
    in_use = counts + low_counts
    caps = (FIRST_SLOTS, 1)
    term_extra, term_passed, term_landed, term_misses = route(
        me, term_table, 0, TERM_SPARE, in_use, jnp.zeros_like(in_use), caps, tag, span, True
    )
    term_fits = (term_misses == 0) & (jnp.max(term_counts) <= TERM_SPARE)

    slot_ids = jnp.arange(devices * READ_SLOTS, dtype=jnp.int32)
    via = choose(landed[:, None] == tile_ids, slot_ids[:, None], 0)
    slot = holder * READ_SLOTS + rank
    then_slot = jnp.where(rank < READ_SLOTS, slot, via)
    direct = (rank >= READ_SLOTS) & (rank < 2 * READ_SLOTS)
    now_slot = jnp.where(direct, slot - READ_SLOTS, -1)
    now_rows = pad_rows(slot_rows(now_slot, READ_SLOTS, dens)).reshape(-1, 1)
    then_rows = pad_rows(slot_rows(then_slot, READ_SLOTS, dens)).reshape(-1, 1)
    now_rows, then_rows = lax.optimization_barrier((now_rows, then_rows))

    def read_two_step():
        return pick_rows(
            now_rows,
            received.reshape(-1, lanes),
            swap,
            then_rows,
            received_then.reshape(-1, lanes),
        )

    def read_one_step():
        slots = slot_count(most)
        (whole,) = gather_tiles([requests(0, slots)], density_rows)
        rows = pad_rows(slot_rows(holder * slots + rank, slots, dens))
        return pick_rows(rows, exchange_slots(whole).reshape(-1, lanes), swap)

    tiles = lax.cond(read_fits, read_two_step, read_one_step)
    tiles = tiles.reshape(ROLES, quartet_count, PAD_N, lanes)
    high, low = contract(tiles, integrals, first, second)
    high = high.reshape(tile_count * PAD_N, lanes)
    low = low.reshape(tile_count * PAD_N, lanes)

    def send(term_of_slot, slots):
        per = rows_per_group(slots)
        ids = jnp.arange(dens, dtype=jnp.int32).reshape(1, dens // per, per, 1)
        term = term_of_slot[:, None, None, :]
        rows = jnp.where(term >= 0, term * PAD_N + ids, -1).reshape(-1)
        packed = pack_terms(rows, swap, high, low)
        return exchange_slots(packed.reshape(devices, dens // per, per * slots, lanes))

    to_holder = holder[:, None] == device_ids
    place_ids = jnp.arange(FIRST_SLOTS, dtype=jnp.int32)
    my_low = lax.dynamic_index_in_dim(low_ranks, me, 0, keepdims=False)
    ends = jnp.concatenate([to_holder, to_holder])[:, :, None]
    places = jnp.concatenate([rank, my_low])[:, None, None] == place_ids
    both_ids = jnp.arange(2 * tile_count, dtype=jnp.int32)
    term_of_slot = choose(ends & places, both_ids[:, None, None], 0)
    arrived = send(jnp.maximum(term_of_slot, term_extra), FIRST_SLOTS)
    relayed = hand_on(term_passed, arrived, dens)

    hit = (ranks[:, :, None] == place_ids) | (low_ranks[:, :, None] == place_ids)
    landing = landing_rows(choose(mine[:, :, None] & hit, local_tile[:, :, None], 1), blocks)
    relay_landing = relay_landing_rows(term_landed, FIRST_SLOTS, blocks)
    landing, relay_landing = lax.optimization_barrier((landing, relay_landing))

    def write_two_step():
        return scatter_terms(
            landing, arrived, FIRST_SLOTS, rows_dev, blocks, relay_landing, relayed
        )

    def write_one_step():
        slots = slot_count(most)
        wide = slot_count(2 * slots)
        places = rank[:, None, None] == jnp.arange(slots)
        term_of_slot = choose(to_holder[:, :, None] & places, tile_ids[:, None, None], 0)
        none = jnp.full((devices, wide // 2 - slots), -1, jnp.int32)
        low_term = jnp.where(term_of_slot >= 0, term_of_slot + tile_count, -1)
        whole = send(jnp.concatenate([term_of_slot, none, low_term, none], axis=1), wide)
        wanted = requests(0, slots)
        landing = jnp.concatenate([wanted, none, wanted, none], axis=1)
        return scatter_terms(landing_rows(landing, blocks), whole, wide, rows_dev, blocks)

    fock = lax.cond(term_fits, write_two_step, write_one_step)
    return jnp.transpose(fock, (0, 2, 1, 3))


def solution(mesh):
    return jax.shard_map(
        local,
        mesh=mesh,
        in_specs=(
            P(AXES, None, None),
            P(AXES, None),
            P(AXES, None, None, None),
            P(),
        ),
        out_specs=P(AXES, None, None, None),
        check_vma=False,
    )
```

profile of v0, /device:TPU:0, one launch (start us, length us, event | category | flops | bytes accessed | tf_op | source)
XLA Modules:
  0.0 287.1 jit_solution(15828028307415265796)
XLA Ops:
  4.3 7.3 %all-to-all-start.2 = ((s32[32,1,128]{2,1,0:T(1,128)}), s32[32,1,128]{2,1,0:T(1,128)S(1)}, u32[]{:S(2)}, u32[]{:S(2)}) async-start(s32[32,1,128]{2,1,0:T(1,128)} %broadcast_in_dim.385), calls=%async_computation.2 | async-start | bytes 32768 | tf_op jit(solution)/shard_map/all_to_all | solution.py:574
  12.8 5.9 %all-to-all-done.2 = s32[32,1,128]{2,1,0:T(1,128)S(1)} async-done(((s32[32,1,128]{2,1,0:T(1,128)}), s32[32,1,128]{2,1,0:T(1,128)S(1)}, u32[]{:S(2)}, u32[]{:S(2)}) %all-to-all-start.2) | async-done | bytes 16416 | tf_op jit(solution)/shard_map/all_to_all | solution.py:574
  19.6 4.9 %route.2 = (s32[257]{0:T(512)}, s32[64]{0:T(128)}, s32[64]{0:T(128)}, s32[64]{0:T(128)}) custom-call(s32[1]{0:T(128)} %bitcast.8.me_ref, s32[32,128]{1,0:T(8,128)} %bitcast.52, s32[2048]{0:T(1024)} %reshape.1250.state_hbm), custom_call_target="tpu_custom_call" | custom-call | tf_op jit(solution)/shard_map/route/pallas_call | solution.py:504
  28.0 10.8 %gather_tiles.3 = (bf16[32,3,8,1024]{3,2,1,0:T(8,128)(2,1)}, bf16[32,3,8,1024]{3,2,1,0:T(8,128)(2,1)}) custom-call(s32[512,1]{1,0:T(8,128)} %copy.39.target_ref, bf16[4,12,128,1024]{3,2,1,0:T(8,128)(2,1)} %bitcast.38), custom_call_target="tpu_custom_call" | custom-call | tf_op jit(solution)/shard_map/gather_tiles/pallas_call | solution.py:106
  38.8 3.4 %all-to-all-start.3 = ((bf16[32,3,8,1024]{3,2,1,0:T(8,128)(2,1)}), bf16[32,3,8,1024]{3,2,1,0:T(8,128)(2,1)}, u32[]{:S(2)}, u32[]{:S(2)}) async-start(bf16[32,3,8,1024]{3,2,1,0:T(8,128)(2,1)} %get-tuple-element.141), calls=%async_computation.3 | async-start | bytes 3145728 | tf_op jit(solution)/shard_map/all_to_all | solution.py:574
  43.1 27.1 %regroup.2 = (bf16[8,1024,1024]{2,1,0:T(8,128)(2,1)}, bf16[8,1024,1024]{2,1,0:T(8,128)(2,1)}) custom-call(bf16[1024,1024]{1,0:T(8,128)(2,1)S(1)} %fusion.12.swap_ref, bf16[512,512]{1,0:T(8,128)(2,1)} %fusion.13.trade_ref, bf16[8,1024,1024]{2,1,0:T(8,128)(2,1)} %block_ref.5), custom_call_target="tpu_custom_call" | custom-call | flops 10737418240 | bytes 10737418240 | tf_op jit(solution)/shard_map/regroup/pallas_call | solution.py:256
  75.5 4.5 %all-to-all-done.3 = bf16[32,3,8,1024]{3,2,1,0:T(8,128)(2,1)} async-done(((bf16[32,3,8,1024]{3,2,1,0:T(8,128)(2,1)}), bf16[32,3,8,1024]{3,2,1,0:T(8,128)(2,1)}, u32[]{:S(2)}, u32[]{:S(2)}) %all-to-all-start.3) | async-done | bytes 1572896 | tf_op jit(solution)/shard_map/all_to_all | solution.py:574
  80.0 4.6 %pick_rows.6 = bf16[768,1024]{1,0:T(8,128)(2,1)} custom-call(bf16[768,1024]{1,0:T(8,128)(2,1)} %bitcast.49, s32[768,1]{1,0:T(8,128)} %select_n.668.refs_1_, bf16[768,1024]{1,0:T(8,128)(2,1)} %bitcast.17.refs_2_), custom_call_target="tpu_custom_call" | custom-call | tf_op jit(solution)/shard_map/pick_rows/pallas_call | solution.py:185
  85.6 3.9 %all-to-all-start.4 = ((bf16[32,3,8,1024]{3,2,1,0:T(8,128)(2,1)}), bf16[32,3,8,1024]{3,2,1,0:T(8,128)(2,1)}, u32[]{:S(2)}, u32[]{:S(2)}) async-start(bf16[32,3,8,1024]{3,2,1,0:T(8,128)(2,1)} %bitcast.48), calls=%async_computation.4 | async-start | bytes 3145728 | tf_op jit(solution)/shard_map/all_to_all | solution.py:574
  89.5 17.6 %regroup.3 = (bf16[8,1024,1024]{2,1,0:T(8,128)(2,1)}, bf16[8,1024,1024]{2,1,0:T(8,128)(2,1)}) custom-call(bf16[1024,1024]{1,0:T(8,128)(2,1)S(1)} %fusion.12.swap_ref, bf16[512,512]{1,0:T(8,128)(2,1)} %fusion.13.trade_ref, bf16[8,1024,1024]{2,1,0:T(8,128)(2,1)} %block_ref.5, ...), custom_call_target="tpu_custom_call", output_to_operand_aliasing={{0}: (3, {}), {1}: (4, {})} | custom-call | flops 1 | bytes 1 | tf_op jit(solution)/shard_map/regroup/pallas_call | solution.py:256
  111.5 6.6 %route.3 = (s32[513]{0:T(1024)}, s32[128]{0:T(128)}, s32[32]{0:T(128)}, s32[32]{0:T(128)}) custom-call(s32[1]{0:T(128)} %bitcast.8.me_ref, s32[32,17]{1,0:T(8,128)} %pad_add_fusion.3.list_ref, s32[2048]{0:T(1024)} %reshape.1254.state_hbm), custom_call_target="tpu_custom_call" | custom-call | tf_op jit(solution)/shard_map/route/pallas_call | solution.py:504
  120.7 6.3 %all-to-all-done.4 = bf16[32,3,8,1024]{3,2,1,0:T(8,128)(2,1)} async-done(((bf16[32,3,8,1024]{3,2,1,0:T(8,128)(2,1)}), bf16[32,3,8,1024]{3,2,1,0:T(8,128)(2,1)}, u32[]{:S(2)}, u32[]{:S(2)}) %all-to-all-start.4) | async-done | bytes 1572896 | tf_op jit(solution)/shard_map/all_to_all | solution.py:574
  127.0 8.6 %conditional.2 = (bf16[6,8,16,1024]{3,2,1,0:T(8,128)(2,1)}) conditional(s32[]{:T(128)} %convert_element_type.63, (s32[48]{0:T(128)S(1)}, s32[48]{0:T(128)S(1)}, pred[48]{0:T(512)(128)(4,1)S(1)}, s32[48]{0:T(128)S(1)}, s32[48]{0:T(128)S(1)}, /*index=5*/s32[48]{0:T(128)S(1)}, pred[32,48]{1,0:T(8,128)(4,1)S(1)}, s32[32,48]{1,0:T(8,128)S(1)}, ...), branch_computations={%region_17.19_spmd, %region_19.20_spmd} | conditional | flops 61034 | bytes 18928204 | solution.py:689
  128.9 6.7 %pick_rows.5 = bf16[768,1024]{1,0:T(8,128)(2,1)} custom-call(s32[768,1]{1,0:T(8,128)} %copy.42.refs_0_, bf16[768,1024]{1,0:T(8,128)(2,1)} %bitcast.2.refs_1_, bf16[1024,1024]{1,0:T(8,128)(2,1)S(1)} %get-tuple-element.97.refs_2_, s32[768,1]{1,0:T(8,128)} %copy.43.refs_3_, bf16[768,1024]{1,0:T(8,128)(2,1)} %bitcast.3.refs_4_), custom_call_target="tpu_custom_call" | custom-call | tf_op jit(solution)/shard_map/cond/branch_1_fun/pick_rows/pallas_call | solution.py:185
  135.6 25.7 %contract.1 = (bf16[6,8,16,1024]{3,2,1,0:T(8,128)(2,1)S(1)}, bf16[6,8,16,1024]{3,2,1,0:T(8,128)(2,1)}) custom-call(bf16[6,8,16,1024]{3,2,1,0:T(8,128)(2,1)} %get-tuple-element.241.tiles_ref, bf16[8,1024,1024]{2,1,0:T(8,128)(2,1)} %block_ref.5, bf16[8,1024,1024]{2,1,0:T(8,128)(2,1)} %get-tuple-element.158.first_ref, ...), custom_call_target="tpu_custom_call" | custom-call | tf_op jit(solution)/shard_map/contract/pallas_call | solution.py:300
  161.4 10.9 %pack_terms.3 = bf16[1536,1024]{1,0:T(8,128)(2,1)} custom-call(s32[1536,1]{1,0:T(8,128)} %select_n.669.target_ref, bf16[1024,1024]{1,0:T(8,128)(2,1)S(1)} %fusion.12.swap_ref, bf16[768,1024]{1,0:T(8,128)(2,1)S(1)} %bitcast.44, bf16[768,1024]{1,0:T(8,128)(2,1)} %bitcast.46), custom_call_target="tpu_custom_call" | custom-call | tf_op jit(solution)/shard_map/pack_terms/pallas_call | solution.py:330
  172.3 3.9 %all-to-all-start.5 = ((bf16[32,3,16,1024]{3,2,1,0:T(8,128)(2,1)}), bf16[32,3,16,1024]{3,2,1,0:T(8,128)(2,1)}, u32[]{:S(2)}, u32[]{:S(2)}) async-start(bf16[32,3,16,1024]{3,2,1,0:T(8,128)(2,1)} %bitcast.41), calls=%async_computation.5 | async-start | bytes 6291456 | tf_op jit(solution)/shard_map/all_to_all | solution.py:574
  176.4 1.3 slice.44
  180.7 66.8 %all-to-all-done.5 = bf16[32,3,16,1024]{3,2,1,0:T(8,128)(2,1)} async-done(((bf16[32,3,16,1024]{3,2,1,0:T(8,128)(2,1)}), bf16[32,3,16,1024]{3,2,1,0:T(8,128)(2,1)}, u32[]{:S(2)}, u32[]{:S(2)}) %all-to-all-start.5) | async-done | bytes 3145760 | tf_op jit(solution)/shard_map/all_to_all | solution.py:574
  247.5 4.4 %pick_rows.7 = bf16[32,3,4,1024]{3,2,1,0:T(4,128)(2,1)} custom-call(s32[384,1]{1,0:T(8,128)} %select_n.670.refs_0_, bf16[1536,1024]{1,0:T(8,128)(2,1)} %bitcast.26.refs_1_), custom_call_target="tpu_custom_call" | custom-call | tf_op jit(solution)/shard_map/pick_rows/pallas_call | solution.py:185
  251.9 4.0 %all-to-all-start.6 = ((bf16[32,3,4,1024]{3,2,1,0:T(4,128)(2,1)}), bf16[32,3,4,1024]{3,2,1,0:T(4,128)(2,1)S(1)}, u32[]{:S(2)}, u32[]{:S(2)}) async-start(bf16[32,3,4,1024]{3,2,1,0:T(4,128)(2,1)} %pick_rows.7), calls=%async_computation.6 | async-start | bytes 1572864 | tf_op jit(solution)/shard_map/all_to_all | solution.py:574
  256.8 19.7 %all-to-all-done.6 = bf16[32,3,4,1024]{3,2,1,0:T(4,128)(2,1)S(1)} async-done(((bf16[32,3,4,1024]{3,2,1,0:T(4,128)(2,1)}), bf16[32,3,4,1024]{3,2,1,0:T(4,128)(2,1)S(1)}, u32[]{:S(2)}, u32[]{:S(2)}) %all-to-all-start.6) | async-done | bytes 786464 | tf_op jit(solution)/shard_map/all_to_all | solution.py:574
  276.5 10.6 %conditional.3 = (bf16[4,12,128,1024]{3,2,1,0:T(8,128)(2,1)}) conditional(s32[]{:T(128)} %convert_element_type.62, (pred[32,48]{1,0:T(8,128)(4,1)S(1)}, s32[32,48]{1,0:T(8,128)S(1)}, s32[32,48]{1,0:T(8,128)S(1)}, pred[48,32]{0,1:T(8,128)(4,1)S(1)}, s32[48]{0:T(128)S(1)}, /*index=5*/s32[48]{0:T(128)S(1)}, bf16[1024,1024]{1,0:T(8,128)(2,1)S(1)}, ...), branch_computations={%region_22.25_spmd, %region_25.26_spmd} | conditional | flops 115376 | bytes 37879336 | solution.py:735
  276.5 10.6 %scatter_terms.3 = bf16[4,12,128,1024]{3,2,1,0:T(8,128)(2,1)} custom-call(s32[2,128]{1,0:T(2,128)S(1)} %get-tuple-element.109.refs_0_, bf16[32,3,4,1024]{3,2,1,0:T(4,128)(2,1)S(1)} %get-tuple-element.110.refs_1_, s32[1,256]{1,0:T(1,128)S(1)} %get-tuple-element.111.refs_2_, bf16[32,6,8,1024]{3,2,1,0:T(8,128)(2,1)} %bitcast.7.refs_3_), custom_call_target="tpu_custom_call" | custom-call | tf_op jit(solution)/shard_map/cond/branch_1_fun/scatter_terms/pallas_call | solution.py:408
  (145 shorter events, 26.9 us)
Async XLA Ops:
  4.3 14.4 %all-to-all-start.2 = ((s32[32,1,128]{2,1,0:T(1,128)}), s32[32,1,128]{2,1,0:T(1,128)S(1)}, u32[]{:S(2)}, u32[]{:S(2)}) async-start(s32[32,1,128]{2,1,0:T(1,128)} %broadcast_in_dim.385), calls=%async_computation.2 | async-start | bytes 32768 | tf_op jit(solution)/shard_map/all_to_all | solution.py:574
  18.8 0.8 copy-start.1
  38.8 41.2 %all-to-all-start.3 = ((bf16[32,3,8,1024]{3,2,1,0:T(8,128)(2,1)}), bf16[32,3,8,1024]{3,2,1,0:T(8,128)(2,1)}, u32[]{:S(2)}, u32[]{:S(2)}) async-start(bf16[32,3,8,1024]{3,2,1,0:T(8,128)(2,1)} %get-tuple-element.141), calls=%async_computation.3 | async-start | bytes 3145728 | tf_op jit(solution)/shard_map/all_to_all | solution.py:574
  43.1 27.1 %copy-start.6 = (s32[64]{0:T(128)S(1)}, s32[64]{0:T(128)}, u32[]{:S(2)}) copy-start(s32[64]{0:T(128)} %get-tuple-element.147) | copy-start | bytes 772
  43.1 30.4 %copy-start.2 = (s32[32,1,128]{2,1,0:T(1,128)S(1)}, s32[32,1,128]{2,1,0:T(1,128)}, u32[]{:S(2)}) copy-start(s32[32,1,128]{2,1,0:T(1,128)} %copy-done.1) | copy-start | bytes 49156
  43.1 31.9 %copy-start.5 = (s32[64]{0:T(128)S(1)}, s32[64]{0:T(128)}, u32[]{:S(2)}) copy-start(s32[64]{0:T(128)} %get-tuple-element.153) | copy-start | bytes 772
  85.6 41.4 %all-to-all-start.4 = ((bf16[32,3,8,1024]{3,2,1,0:T(8,128)(2,1)}), bf16[32,3,8,1024]{3,2,1,0:T(8,128)(2,1)}, u32[]{:S(2)}, u32[]{:S(2)}) async-start(bf16[32,3,8,1024]{3,2,1,0:T(8,128)(2,1)} %bitcast.48), calls=%async_computation.4 | async-start | bytes 3145728 | tf_op jit(solution)/shard_map/all_to_all | solution.py:574
  161.4 10.9 %copy-start = (bf16[6,8,16,1024]{3,2,1,0:T(8,128)(2,1)}, bf16[6,8,16,1024]{3,2,1,0:T(8,128)(2,1)S(1)}, u32[]{:S(2)}) copy-start(bf16[6,8,16,1024]{3,2,1,0:T(8,128)(2,1)S(1)} %get-tuple-element.160) | copy-start | bytes 4718596
  172.3 7.3 %copy-start.4 = (s32[32]{0:T(128)S(1)}, s32[32]{0:T(128)}, u32[]{:S(2)}) copy-start(s32[32]{0:T(128)} %get-tuple-element.165) | copy-start | bytes 388
  172.3 75.2 %all-to-all-start.5 = ((bf16[32,3,16,1024]{3,2,1,0:T(8,128)(2,1)}), bf16[32,3,16,1024]{3,2,1,0:T(8,128)(2,1)}, u32[]{:S(2)}, u32[]{:S(2)}) async-start(bf16[32,3,16,1024]{3,2,1,0:T(8,128)(2,1)} %bitcast.41), calls=%async_computation.5 | async-start | bytes 6291456 | tf_op jit(solution)/shard_map/all_to_all | solution.py:574
  176.2 80.2 %copy-start.3 = (s32[32]{0:T(128)S(1)}, s32[32]{0:T(128)}, u32[]{:S(2)}) copy-start(s32[32]{0:T(128)} %get-tuple-element.163) | copy-start | bytes 388
  251.9 24.6 %all-to-all-start.6 = ((bf16[32,3,4,1024]{3,2,1,0:T(4,128)(2,1)}), bf16[32,3,4,1024]{3,2,1,0:T(4,128)(2,1)S(1)}, u32[]{:S(2)}, u32[]{:S(2)}) async-start(bf16[32,3,4,1024]{3,2,1,0:T(4,128)(2,1)} %pick_rows.7), calls=%async_computation.6 | async-start | bytes 1572864 | tf_op jit(solution)/shard_map/all_to_all | solution.py:574
where the time goes:
time: 289 us; the launch traced here: 287 us
  Pallas kernels  130 us (45%)
  waiting for transfers between devices  103 us (36%)
  starting transfers between devices  22.5 us (8%)
  local copies, waits for them, and re-layouts  15.1 us (5%)
  other arithmetic  13 us (4%)
  between operations  3.24 us (1%)
    all_to_all x5, waiting for transfers between devices, exchange_slots(): lax.all_to_all(array, AXES, split_axis=axis, concat_axis=axis, tiled=True)  103 us
    pallas_call x2, Pallas kernels, regroup(): pl.pallas_call(functools.partial(regroup_body, width=width), grid=(end -...  44.7 us
    pallas_call x1, Pallas kernels, contract(): pl.pallas_call(contract_body, grid=(count,), in_specs=[part, whole, whole...  25.7 us
    all_to_all x5, starting transfers between devices, exchange_slots(): lax.all_to_all(array, AXES, split_axis=axis, concat_axis=axis, tiled=True)  22.5 us
    pallas_call x3, Pallas kernels, pick_rows(): pl.pallas_call(functools.partial(pick_body, relay=relayed is not None, sw...  15.7 us
    pallas_call x2, Pallas kernels, route(): pl.pallas_call(functools.partial(route_body, spare=spare, begin=begin, ta...  11.5 us
    pallas_call x1, Pallas kernels, pack_terms(): pl.pallas_call(pack_body, grid=(count // chunk,), in_specs=[pl.BlockSpec(...  10.9 us
    pallas_call x1, Pallas kernels, gather_tiles(): pl.pallas_call(gather_body, grid=(groups,), in_specs=[pl.BlockSpec(target...  10.8 us
  transfers between devices with their start and end apart: 5, of which 5 were waited for; matrix products, arithmetic and copies ran while one was open for 6% of the time, Pallas kernels for 18%

commit v1 on v0

--- a/solution.py
+++ b/solution.py
@@ -326,7 +326,7 @@
 def pack_terms(row_of, swap, high, low):
     count = row_of.shape[0]
     half, lanes = high.shape
-    chunk = math.gcd(count, 256 if count <= 2048 else 64)
+    chunk = math.gcd(count, 512 if count <= 2048 else 64)
     return pl.pallas_call(
         pack_body,
         grid=(count // chunk,),
@@ -669,16 +669,14 @@
     now_slot = jnp.where(direct, slot - READ_SLOTS, -1)
     now_rows = pad_rows(slot_rows(now_slot, READ_SLOTS, dens)).reshape(-1, 1)
     then_rows = pad_rows(slot_rows(then_slot, READ_SLOTS, dens)).reshape(-1, 1)
-    now_rows, then_rows = lax.optimization_barrier((now_rows, then_rows))
-
-    def read_two_step():
-        return pick_rows(
-            now_rows,
-            received.reshape(-1, lanes),
-            swap,
-            then_rows,
-            received_then.reshape(-1, lanes),
-        )
+
+    two_step = pick_rows(
+        now_rows,
+        received.reshape(-1, lanes),
+        swap,
+        then_rows,
+        received_then.reshape(-1, lanes),
+    )
 
     def read_one_step():
         slots = slot_count(most)
@@ -686,7 +684,7 @@
         rows = pad_rows(slot_rows(holder * slots + rank, slots, dens))
         return pick_rows(rows, exchange_slots(whole).reshape(-1, lanes), swap)
 
-    tiles = lax.cond(read_fits, read_two_step, read_one_step)
+    tiles = lax.cond(read_fits, lambda: two_step, read_one_step)
     tiles = tiles.reshape(ROLES, quartet_count, PAD_N, lanes)
     high, low = contract(tiles, integrals, first, second)
     high = high.reshape(tile_count * PAD_N, lanes)

time: 289 us -> 286 us (0.990)
  no operation moved by 1% of the time
where the time goes in v1:
time: 286 us; the launch traced here: 284 us
  Pallas kernels  129 us (45%)
  waiting for transfers between devices  103 us (36%)
  starting transfers between devices  22.5 us (8%)
  local copies, waits for them, and re-layouts  14.8 us (5%)
  other arithmetic  12.9 us (5%)
  between operations  3.04 us (1%)
    all_to_all x5, waiting for transfers between devices, exchange_slots(): lax.all_to_all(array, AXES, split_axis=axis, concat_axis=axis, tiled=True)  103 us
    pallas_call x2, Pallas kernels, regroup(): pl.pallas_call(functools.partial(regroup_body, width=width), grid=(end -...  44.7 us
    pallas_call x1, Pallas kernels, contract(): pl.pallas_call(contract_body, grid=(count,), in_specs=[part, whole, whole...  25.7 us
    all_to_all x5, starting transfers between devices, exchange_slots(): lax.all_to_all(array, AXES, split_axis=axis, concat_axis=axis, tiled=True)  22.5 us
    pallas_call x3, Pallas kernels, pick_rows(): pl.pallas_call(functools.partial(pick_body, relay=relayed is not None, sw...  15.7 us
    pallas_call x1, Pallas kernels, gather_tiles(): pl.pallas_call(gather_body, grid=(groups,), in_specs=[pl.BlockSpec(target...  10.8 us
    pallas_call x2, Pallas kernels, route(): pl.pallas_call(functools.partial(route_body, spare=spare, begin=begin, ta...  10.7 us
    pallas_call x1, Pallas kernels, scatter_terms(): pl.pallas_call(functools.partial(scatter_body, relay=relayed is not None)...  10.6 us
  transfers between devices with their start and end apart: 5, of which 5 were waited for; matrix products, arithmetic and copies ran while one was open for 6% of the time, Pallas kernels for 18%

profile of v1, /device:TPU:0, one launch (start us, length us, event | category | flops | bytes accessed | tf_op | source)
XLA Modules:
  0.0 284.4 jit_solution(14644893356286858301)
XLA Ops:
  4.3 7.3 %all-to-all-start.2 = ((s32[32,1,128]{2,1,0:T(1,128)}), s32[32,1,128]{2,1,0:T(1,128)S(1)}, u32[]{:S(2)}, u32[]{:S(2)}) async-start(s32[32,1,128]{2,1,0:T(1,128)} %broadcast_in_dim.385), calls=%async_computation.2 | async-start | bytes 32768 | tf_op jit(solution)/shard_map/all_to_all | solution.py:574
  12.8 5.9 %all-to-all-done.2 = s32[32,1,128]{2,1,0:T(1,128)S(1)} async-done(((s32[32,1,128]{2,1,0:T(1,128)}), s32[32,1,128]{2,1,0:T(1,128)S(1)}, u32[]{:S(2)}, u32[]{:S(2)}) %all-to-all-start.2) | async-done | bytes 16416 | tf_op jit(solution)/shard_map/all_to_all | solution.py:574
  19.6 4.7 %route.2 = (s32[257]{0:T(512)}, s32[64]{0:T(128)}, s32[64]{0:T(128)}, s32[64]{0:T(128)}) custom-call(s32[1]{0:T(128)} %bitcast.6.me_ref, s32[32,128]{1,0:T(8,128)} %bitcast.51, s32[2048]{0:T(1024)} %reshape.1248.state_hbm), custom_call_target="tpu_custom_call" | custom-call | tf_op jit(solution)/shard_map/route/pallas_call | solution.py:504
  27.7 10.8 %gather_tiles.3 = (bf16[32,3,8,1024]{3,2,1,0:T(8,128)(2,1)}, bf16[32,3,8,1024]{3,2,1,0:T(8,128)(2,1)}) custom-call(s32[512,1]{1,0:T(8,128)} %copy.39.target_ref, bf16[4,12,128,1024]{3,2,1,0:T(8,128)(2,1)} %bitcast.37), custom_call_target="tpu_custom_call" | custom-call | tf_op jit(solution)/shard_map/gather_tiles/pallas_call | solution.py:106
  38.5 3.4 %all-to-all-start.3 = ((bf16[32,3,8,1024]{3,2,1,0:T(8,128)(2,1)}), bf16[32,3,8,1024]{3,2,1,0:T(8,128)(2,1)}, u32[]{:S(2)}, u32[]{:S(2)}) async-start(bf16[32,3,8,1024]{3,2,1,0:T(8,128)(2,1)} %get-tuple-element.126), calls=%async_computation.3 | async-start | bytes 3145728 | tf_op jit(solution)/shard_map/all_to_all | solution.py:574
  42.8 27.1 %regroup.2 = (bf16[8,1024,1024]{2,1,0:T(8,128)(2,1)}, bf16[8,1024,1024]{2,1,0:T(8,128)(2,1)}) custom-call(bf16[1024,1024]{1,0:T(8,128)(2,1)S(1)} %fusion.12.swap_ref.refs_2_, bf16[512,512]{1,0:T(8,128)(2,1)} %fusion.13.trade_ref, bf16[8,1024,1024]{2,1,0:T(8,128)(2,1)} %block_ref.5), custom_call_target="tpu_custom_call" | custom-call | flops 10737418240 | bytes 10737418240 | tf_op jit(solution)/shard_map/regroup/pallas_call | solution.py:256
  76.6 3.1 %all-to-all-done.3 = bf16[32,3,8,1024]{3,2,1,0:T(8,128)(2,1)} async-done(((bf16[32,3,8,1024]{3,2,1,0:T(8,128)(2,1)}), bf16[32,3,8,1024]{3,2,1,0:T(8,128)(2,1)}, u32[]{:S(2)}, u32[]{:S(2)}) %all-to-all-start.3) | async-done | bytes 1572896 | tf_op jit(solution)/shard_map/all_to_all | solution.py:574
  79.7 4.6 %pick_rows.5 = bf16[768,1024]{1,0:T(8,128)(2,1)} custom-call(bf16[768,1024]{1,0:T(8,128)(2,1)} %bitcast.48, s32[768,1]{1,0:T(8,128)} %select_n.668.refs_1_, bf16[768,1024]{1,0:T(8,128)(2,1)} %bitcast.15.refs_2_.refs_4_), custom_call_target="tpu_custom_call" | custom-call | tf_op jit(solution)/shard_map/pick_rows/pallas_call | solution.py:185
  85.3 3.9 %all-to-all-start.4 = ((bf16[32,3,8,1024]{3,2,1,0:T(8,128)(2,1)}), bf16[32,3,8,1024]{3,2,1,0:T(8,128)(2,1)}, u32[]{:S(2)}, u32[]{:S(2)}) async-start(bf16[32,3,8,1024]{3,2,1,0:T(8,128)(2,1)} %bitcast.47), calls=%async_computation.4 | async-start | bytes 3145728 | tf_op jit(solution)/shard_map/all_to_all | solution.py:574
  89.2 17.6 %regroup.3 = (bf16[8,1024,1024]{2,1,0:T(8,128)(2,1)}, bf16[8,1024,1024]{2,1,0:T(8,128)(2,1)}) custom-call(bf16[1024,1024]{1,0:T(8,128)(2,1)S(1)} %fusion.12.swap_ref.refs_2_, bf16[512,512]{1,0:T(8,128)(2,1)} %fusion.13.trade_ref, bf16[8,1024,1024]{2,1,0:T(8,128)(2,1)} %block_ref.5, ...), custom_call_target="tpu_custom_call", output_to_operand_aliasing={{0}: (3, {}), {1}: (4, {})} | custom-call | flops 1 | bytes 1 | tf_op jit(solution)/shard_map/regroup/pallas_call | solution.py:256
  111.2 6.0 %route.3 = (s32[513]{0:T(1024)}, s32[128]{0:T(128)}, s32[32]{0:T(128)}, s32[32]{0:T(128)}) custom-call(s32[1]{0:T(128)} %bitcast.6.me_ref, s32[32,17]{1,0:T(8,128)} %pad_add_fusion.3.list_ref, s32[2048]{0:T(1024)} %reshape.1252.state_hbm), custom_call_target="tpu_custom_call" | custom-call | tf_op jit(solution)/shard_map/route/pallas_call | solution.py:504
  118.5 1.2 select_n.669.target_ref
  119.7 7.0 %all-to-all-done.4 = bf16[32,3,8,1024]{3,2,1,0:T(8,128)(2,1)} async-done(((bf16[32,3,8,1024]{3,2,1,0:T(8,128)(2,1)}), bf16[32,3,8,1024]{3,2,1,0:T(8,128)(2,1)}, u32[]{:S(2)}, u32[]{:S(2)}) %all-to-all-start.4) | async-done | bytes 1572896 | tf_op jit(solution)/shard_map/all_to_all | solution.py:574
  126.7 6.7 %pick_rows.6 = bf16[768,1024]{1,0:T(8,128)(2,1)} custom-call(s32[768,1]{1,0:T(8,128)} %reshape_reshape.11.refs_0_, bf16[768,1024]{1,0:T(8,128)(2,1)} %bitcast.20.refs_1_, bf16[1024,1024]{1,0:T(8,128)(2,1)S(1)} %fusion.12.swap_ref.refs_2_, s32[768,1]{1,0:T(8,128)} %reshape_reshape.12.refs_3_, bf16[768,1024]{1,0:T(8,128)(2,1)} %bitcast.15.refs_2_.refs_4_), custom_call_target="tpu_custom_call" | custom-call | tf_op jit(solution)/shard_map/pick_rows/pallas_call | solution.py:185
  133.4 25.7 %contract.1 = (bf16[6,8,16,1024]{3,2,1,0:T(8,128)(2,1)S(1)}, bf16[6,8,16,1024]{3,2,1,0:T(8,128)(2,1)}) custom-call(bf16[6,8,16,1024]{3,2,1,0:T(8,128)(2,1)} %get-tuple-element.209.tiles_ref, bf16[8,1024,1024]{2,1,0:T(8,128)(2,1)} %block_ref.5, bf16[8,1024,1024]{2,1,0:T(8,128)(2,1)} %get-tuple-element.141.first_ref, ...), custom_call_target="tpu_custom_call" | custom-call | tf_op jit(solution)/shard_map/contract/pallas_call | solution.py:300
  159.2 10.4 %pack_terms.3 = bf16[1536,1024]{1,0:T(8,128)(2,1)} custom-call(s32[1536,1]{1,0:T(8,128)} %select_n.669.target_ref, bf16[1024,1024]{1,0:T(8,128)(2,1)S(1)} %fusion.12.swap_ref.refs_2_, bf16[768,1024]{1,0:T(8,128)(2,1)S(1)} %bitcast.43, bf16[768,1024]{1,0:T(8,128)(2,1)} %bitcast.45), custom_call_target="tpu_custom_call" | custom-call | tf_op jit(solution)/shard_map/pack_terms/pallas_call | solution.py:330
  169.6 3.9 %all-to-all-start.5 = ((bf16[32,3,16,1024]{3,2,1,0:T(8,128)(2,1)}), bf16[32,3,16,1024]{3,2,1,0:T(8,128)(2,1)}, u32[]{:S(2)}, u32[]{:S(2)}) async-start(bf16[32,3,16,1024]{3,2,1,0:T(8,128)(2,1)} %bitcast.40), calls=%async_computation.5 | async-start | bytes 6291456 | tf_op jit(solution)/shard_map/all_to_all | solution.py:574
  173.6 1.2 slice.44
  177.9 66.8 %all-to-all-done.5 = bf16[32,3,16,1024]{3,2,1,0:T(8,128)(2,1)} async-done(((bf16[32,3,16,1024]{3,2,1,0:T(8,128)(2,1)}), bf16[32,3,16,1024]{3,2,1,0:T(8,128)(2,1)}, u32[]{:S(2)}, u32[]{:S(2)}) %all-to-all-start.5) | async-done | bytes 3145760 | tf_op jit(solution)/shard_map/all_to_all | solution.py:574
  244.8 4.4 %pick_rows.7 = bf16[32,3,4,1024]{3,2,1,0:T(4,128)(2,1)} custom-call(s32[384,1]{1,0:T(8,128)} %select_n.670.refs_0_, bf16[1536,1024]{1,0:T(8,128)(2,1)} %bitcast.25.refs_1_), custom_call_target="tpu_custom_call" | custom-call | tf_op jit(solution)/shard_map/pick_rows/pallas_call | solution.py:185
  249.1 4.0 %all-to-all-start.6 = ((bf16[32,3,4,1024]{3,2,1,0:T(4,128)(2,1)}), bf16[32,3,4,1024]{3,2,1,0:T(4,128)(2,1)S(1)}, u32[]{:S(2)}, u32[]{:S(2)}) async-start(bf16[32,3,4,1024]{3,2,1,0:T(4,128)(2,1)} %pick_rows.7), calls=%async_computation.6 | async-start | bytes 1572864 | tf_op jit(solution)/shard_map/all_to_all | solution.py:574
  254.0 19.7 %all-to-all-done.6 = bf16[32,3,4,1024]{3,2,1,0:T(4,128)(2,1)S(1)} async-done(((bf16[32,3,4,1024]{3,2,1,0:T(4,128)(2,1)}), bf16[32,3,4,1024]{3,2,1,0:T(4,128)(2,1)S(1)}, u32[]{:S(2)}, u32[]{:S(2)}) %all-to-all-start.6) | async-done | bytes 786464 | tf_op jit(solution)/shard_map/all_to_all | solution.py:574
  273.7 10.6 %conditional.3 = (bf16[4,12,128,1024]{3,2,1,0:T(8,128)(2,1)}) conditional(s32[]{:T(128)} %convert_element_type.62, (pred[32,48]{1,0:T(8,128)(4,1)S(1)}, s32[32,48]{1,0:T(8,128)S(1)}, s32[32,48]{1,0:T(8,128)S(1)}, pred[48,32]{0,1:T(8,128)(4,1)S(1)}, s32[48]{0:T(128)S(1)}, /*index=5*/s32[48]{0:T(128)S(1)}, bf16[1024,1024]{1,0:T(8,128)(2,1)S(1)}, ...), branch_computations={%region_22.25_spmd, %region_25.26_spmd} | conditional | flops 115376 | bytes 37879336 | solution.py:733
  273.7 10.6 %scatter_terms.3 = bf16[4,12,128,1024]{3,2,1,0:T(8,128)(2,1)} custom-call(s32[2,128]{1,0:T(2,128)S(1)} %get-tuple-element.96.refs_0_, bf16[32,3,4,1024]{3,2,1,0:T(4,128)(2,1)S(1)} %get-tuple-element.97.refs_1_, s32[1,256]{1,0:T(1,128)S(1)} %get-tuple-element.98.refs_2_, bf16[32,6,8,1024]{3,2,1,0:T(8,128)(2,1)} %bitcast.5.refs_3_), custom_call_target="tpu_custom_call" | custom-call | tf_op jit(solution)/shard_map/cond/branch_1_fun/scatter_terms/pallas_call | solution.py:408
  (143 shorter events, 25.2 us)
Async XLA Ops:
  4.3 14.4 %all-to-all-start.2 = ((s32[32,1,128]{2,1,0:T(1,128)}), s32[32,1,128]{2,1,0:T(1,128)S(1)}, u32[]{:S(2)}, u32[]{:S(2)}) async-start(s32[32,1,128]{2,1,0:T(1,128)} %broadcast_in_dim.385), calls=%async_computation.2 | async-start | bytes 32768 | tf_op jit(solution)/shard_map/all_to_all | solution.py:574
  18.8 0.8 copy-start.1
  38.5 41.2 %all-to-all-start.3 = ((bf16[32,3,8,1024]{3,2,1,0:T(8,128)(2,1)}), bf16[32,3,8,1024]{3,2,1,0:T(8,128)(2,1)}, u32[]{:S(2)}, u32[]{:S(2)}) async-start(bf16[32,3,8,1024]{3,2,1,0:T(8,128)(2,1)} %get-tuple-element.126), calls=%async_computation.3 | async-start | bytes 3145728 | tf_op jit(solution)/shard_map/all_to_all | solution.py:574
  42.8 27.2 %copy-start.6 = (s32[64]{0:T(128)S(1)}, s32[64]{0:T(128)}, u32[]{:S(2)}) copy-start(s32[64]{0:T(128)} %get-tuple-element.132) | copy-start | bytes 772
  42.8 30.2 %copy-start.2 = (s32[32,1,128]{2,1,0:T(1,128)S(1)}, s32[32,1,128]{2,1,0:T(1,128)}, u32[]{:S(2)}) copy-start(s32[32,1,128]{2,1,0:T(1,128)} %copy-done.1) | copy-start | bytes 49156
  42.8 31.5 %copy-start.5 = (s32[64]{0:T(128)S(1)}, s32[64]{0:T(128)}, u32[]{:S(2)}) copy-start(s32[64]{0:T(128)} %get-tuple-element.138) | copy-start | bytes 772
  85.3 41.4 %all-to-all-start.4 = ((bf16[32,3,8,1024]{3,2,1,0:T(8,128)(2,1)}), bf16[32,3,8,1024]{3,2,1,0:T(8,128)(2,1)}, u32[]{:S(2)}, u32[]{:S(2)}) async-start(bf16[32,3,8,1024]{3,2,1,0:T(8,128)(2,1)} %bitcast.47), calls=%async_computation.4 | async-start | bytes 3145728 | tf_op jit(solution)/shard_map/all_to_all | solution.py:574
  159.2 10.4 %copy-start = (bf16[6,8,16,1024]{3,2,1,0:T(8,128)(2,1)}, bf16[6,8,16,1024]{3,2,1,0:T(8,128)(2,1)S(1)}, u32[]{:S(2)}) copy-start(bf16[6,8,16,1024]{3,2,1,0:T(8,128)(2,1)S(1)} %get-tuple-element.143) | copy-start | bytes 4718596
  169.6 7.3 %copy-start.4 = (s32[32]{0:T(128)S(1)}, s32[32]{0:T(128)}, u32[]{:S(2)}) copy-start(s32[32]{0:T(128)} %get-tuple-element.148) | copy-start | bytes 388
  169.6 75.2 %all-to-all-start.5 = ((bf16[32,3,16,1024]{3,2,1,0:T(8,128)(2,1)}), bf16[32,3,16,1024]{3,2,1,0:T(8,128)(2,1)}, u32[]{:S(2)}, u32[]{:S(2)}) async-start(bf16[32,3,16,1024]{3,2,1,0:T(8,128)(2,1)} %bitcast.40), calls=%async_computation.5 | async-start | bytes 6291456 | tf_op jit(solution)/shard_map/all_to_all | solution.py:574
  173.4 80.1 %copy-start.3 = (s32[32]{0:T(128)S(1)}, s32[32]{0:T(128)}, u32[]{:S(2)}) copy-start(s32[32]{0:T(128)} %get-tuple-element.146) | copy-start | bytes 388
  249.1 24.6 %all-to-all-start.6 = ((bf16[32,3,4,1024]{3,2,1,0:T(4,128)(2,1)}), bf16[32,3,4,1024]{3,2,1,0:T(4,128)(2,1)S(1)}, u32[]{:S(2)}, u32[]{:S(2)}) async-start(bf16[32,3,4,1024]{3,2,1,0:T(4,128)(2,1)} %pick_rows.7), calls=%async_computation.6 | async-start | bytes 1572864 | tf_op jit(solution)/shard_map/all_to_all | solution.py:574
